TPU v7x, 32 devices: a whole 2x2x4 slice. The times are simulated.
32 devices in a mesh: lat: 4 (over x, core), src: 8 (over z, y).
Axes of the slice: x: 2, y: 2, z: 4, core: 2. Of those that a mesh axis runs over, the one named last changes fastest.
Arguments:
- fine_residual: bfloat16 [8, 16, 256, 2048], P('lat', 'src'), may hold values from -6 to 6
- basis: bfloat16 [8, 16, 2048, 128], P('lat', 'src'), may hold values from -0.25 to 0.25
- diag_inverse: bfloat16 [8, 16, 128, 128], P('lat', 'src'), may hold values from -0.32 to 1.7, as said below
- hoppings: bfloat16 [8, 16, 8, 128, 128], P('lat', 'src'), may hold values from -0.125 to 0.125
- neighbours: int32 [16, 6], replicated, may hold values from 0 to 15, as said below
- aggregation: int32 [8, 16], P('lat', 'src'), may hold values from 0 to 15, as said below
Outputs:
- correction: bfloat16 [8, 16, 256, 2048], P('lat', 'src')
Inputs may be any that keep to these rules, and one draw needn't show every extreme that they name: `diag_inverse`: a site's diagonal inverse is one on the diagonal within a fifth (two fifths in some draws) plus independent off-diagonal entries. The spatial sites form a periodic grid of 8 by 1 by 2 sites, site (x, y, z) having index (x * 1 + y) * 2 + z; columns 2k and 2k+1 hold the two periodic neighbours along grid direction k, one step up and one step down, in an order drawn for each k. `aggregation`: in each row, every aligned block of 2 entries is a permutation of that block's own column indices.
All inputs are finite; a program needn't handle non-finite values.
Results may differ from a plain program's by a relative error of at most 0.0075.
Values may be sent and summed in bfloat16 or wider, within the bound.
A program may use at most 128 MiB of HBM per device.

v0:
```python
import functools

import jax
import jax.numpy as jnp
from jax import lax
from jax.experimental import pallas as pl
from jax.experimental.pallas import tpu as pltpu
from jax.sharding import PartitionSpec as P

SWEEPS = 3
DAMPING = 0.8
CHUNKS = 2
LAG = 4
STORES = 2
F32 = jnp.float32
BF16 = jnp.bfloat16


def dot(a, b):
    return jnp.dot(a, b, preferred_element_type=F32)


def sweep_kernel(
    chunks, lats, srcs, fine, basis, diag, hops, table, agg, last, basis_v,
    fine_v, diag_v, hops_v, rhs, acc, cells, from_partner, from_far, above, below,
    fine_sem, basis_sem, diag_sem, hops_sem,
    partner_send, partner_recv, far_send, far_recv, above_send, above_recv, below_send, below_recv,
):
    times, sites, sources, _ = fine.shape
    rows = sources // chunks
    lat, src = lax.axis_index("lat"), lax.axis_index("src")
    later, earlier = lax.rem(lat + 1, lats), lax.rem(lat + lats - 1, lats)
    odd = lax.rem(src, 2)
    partner = src + 1 - 2 * odd
    far_target = lax.rem(src + 2 - 4 * odd + srcs, srcs)
    far_source = lax.rem(src - 2 + 4 * odd + srcs, srcs)

    barrier = pltpu.get_barrier_semaphore()
    for device in ((later, src), (earlier, src), (lat, partner), (lat, far_source)):
        pl.semaphore_signal(barrier, inc=1, device_id=device, device_id_type=pl.DeviceIdType.MESH)

    def span(c):
        return pl.ds(c * rows, rows)

    def load_fine(c, t, s):
        return pltpu.make_async_copy(
            fine.at[t, s, span(c)], fine_v.at[t, s, span(c)], fine_sem.at[c, t, s])

    def load_basis(t, s):
        return pltpu.make_async_copy(basis.at[t, s], basis_v.at[t, s], basis_sem.at[t, s])

    load_diag = pltpu.make_async_copy(diag, diag_v, diag_sem)
    load_hops = pltpu.make_async_copy(hops, hops_v, hops_sem)

    pieces = [(c, t) for t in range(times) for c in range(chunks)]
    for c, t in pieces:
        for s in range(sites):
            if c == 0:
                load_basis(t, s).start()
            load_fine(c, t, s).start()
        if c == 0 and t == 0:
            load_diag.start()
    load_hops.start()

    def remote(source, target, send, recv, device):
        return pltpu.make_async_remote_copy(
            src_ref=source, dst_ref=target, send_sem=send, recv_sem=recv,
            device_id=device, device_id_type=pl.DeviceIdType.MESH)

    def to_partner(x, c, t):
        return remote(cells.at[x, c, t], from_partner.at[x, c, t],
                      partner_send.at[x, c, t], partner_recv.at[x, c, t], (lat, partner))

    def to_far(x, c, t):
        return remote(from_partner.at[x, c, t], from_far.at[x, c, t],
                      far_send.at[x, c, t], far_recv.at[x, c, t], (lat, far_target))

    def to_later(x, c):
        return remote(cells.at[x, c, times - 1], below.at[x, c],
                      below_send.at[x, c], below_recv.at[x, c], (later, src))

    def to_earlier(x, c):
        return remote(cells.at[x, c, 0], above.at[x, c],
                      above_send.at[x, c], above_recv.at[x, c], (earlier, src))

    def send(x, c, t):
        to_partner(x, c, t).start()
        if t == times - 1:
            to_later(x, c).start()
        if t == 0:
            to_earlier(x, c).start()

    for c, t in pieces:
        for s in range(sites):
            if c == 0:
                load_basis(t, s).wait()
            load_fine(c, t, s).wait()
        if c == 0 and t == 0:
            load_diag.wait()
        coarse = [dot(fine_v[t, s, span(c)], basis_v[t, s]) for s in range(sites)]
        swap = lax.rem(agg[t, 0], sites) == 1
        here = [jnp.where(swap, coarse[1 - s], coarse[s]).astype(BF16) for s in range(sites)]
        applied = [dot(here[s], diag_v[t, s]) for s in range(sites)]
        for s in range(sites):
            cells[0, c, t, s] = (DAMPING * applied[s]).astype(BF16)
            rhs[c, t, s] = here[s]
        if c == 0 and t == 0:
            pl.semaphore_wait(barrier, 4)
        send(0, c, t)
    load_hops.wait()

    def local_terms(x, c, t):
        for s in range(sites):
            own, other = cells[x, c, t, s], cells[x, c, t, 1 - s]
            total = dot(jnp.concatenate([own, own], axis=1), hops_v[t, s, 2:4].reshape(-1, own.shape[1]))
            total += dot(jnp.concatenate([other, other], axis=1), hops_v[t, s, 4:6].reshape(-1, own.shape[1]))
            if t + 1 < times:
                total += dot(cells[x, c, t + 1, s], hops_v[t, s, 6])
            if t > 0:
                total += dot(cells[x, c, t - 1, s], hops_v[t, s, 7])
            acc[c, t, s] = rhs[c, t, s].astype(F32) - total

    def forward(x, c, t):
        to_partner(x, c, t).wait_recv()
        to_far(x, c, t).start()

    def finish(x, c, t):
        if t == times - 1:
            to_earlier(x, c).wait_recv()
        if t == 0:
            to_later(x, c).wait_recv()
        to_far(x, c, t).wait_recv()
        totals = []
        for s in range(sites):
            column = jnp.where(table[0, src * sites + s] == partner * sites + s, 0, 1)
            total = dot(from_partner[x, c, t, s], hops_v[t, s, column])
            total += dot(from_far[x, c, t, s], hops_v[t, s, 1 - column])
            if t == times - 1:
                total += dot(above[x, c, s], hops_v[t, s, 6])
            if t == 0:
                total += dot(below[x, c, s], hops_v[t, s, 7])
            totals.append(total)
        differences = [(acc[c, t, s] - totals[s]).astype(BF16) for s in range(sites)]
        applied = [dot(differences[s], diag_v[t, s]) for s in range(sites)]
        for s in range(sites):
            new = ((1.0 - DAMPING) * cells[x, c, t, s].astype(F32) + DAMPING * applied[s]).astype(BF16)
            if x + 1 < SWEEPS - 1:
                cells[x + 1, c, t, s] = new
            else:
                last[t, s, span(c)] = new
        if x + 1 < SWEEPS - 1:
            send(x + 1, c, t)
            if t == times - 1:
                for each in range(times):
                    local_terms(x + 1, c, each)

    exchanges = SWEEPS - 1
    count = len(pieces)
    for step in range(count + LAG * (2 * exchanges - 1)):
        for x in range(exchanges):
            at = step - 2 * LAG * x
            if 0 <= at < count:
                forward(x, *pieces[at])
                if x == 0:
                    local_terms(0, *pieces[at])
            at -= LAG
            if 0 <= at < count:
                finish(x, *pieces[at])

    for c, t in pieces:
        for x in range(exchanges):
            to_partner(x, c, t).wait_send()
            to_far(x, c, t).wait_send()
            if t == times - 1:
                to_later(x, c).wait_send()
            if t == 0:
                to_earlier(x, c).wait_send()


def prolong_kernel(agg, cells, basis, out, out_v, out_sem):
    times, sites, sources, _ = cells.shape
    blocks = [(t, s, p) for t in range(times) for s in range(sites) for p in range(STORES)]
    rows = sources // STORES

    def store(t, s, p):
        span = pl.ds(p * rows, rows)
        return pltpu.make_async_copy(out_v.at[t, s, span], out.at[t, s, span], out_sem.at[t, s, p])

    for t, s, p in blocks:
        span = pl.ds(p * rows, rows)
        out_v[t, s, span] = lax.dot_general(
            cells[t, lax.rem(agg[t, s], sites), span], basis[t, s], (((1,), (1,)), ((), ())),
            preferred_element_type=F32).astype(BF16)
        store(t, s, p).start()
    for t, s, p in blocks:
        store(t, s, p).wait()


def body(lats, srcs, fine, basis, diag, hops, table, agg):
    times, sites, sources, depth = fine.shape
    width = basis.shape[3]
    chunks, exchanges = CHUNKS, SWEEPS - 1
    rows = sources // chunks
    any_spec = pl.BlockSpec(memory_space=pl.ANY)
    vmem_spec = pl.BlockSpec(memory_space=pltpu.VMEM)
    smem_spec = pl.BlockSpec(memory_space=pltpu.SMEM)
    dma = pltpu.SemaphoreType.DMA
    piece = (sites, rows, width)
    per_piece, per_chunk = dma((exchanges, chunks, times)), dma((exchanges, chunks))
    cells, basis = pl.pallas_call(
        functools.partial(sweep_kernel, chunks, lats, srcs),
        out_shape=[pltpu.VMEM((times, sites, sources, width), BF16), pltpu.VMEM(basis.shape, BF16)],
        in_specs=[any_spec] * 4 + [smem_spec] * 2,
        out_specs=[vmem_spec] * 2,
        scratch_shapes=[
            pltpu.VMEM(fine.shape, BF16),
            pltpu.VMEM(diag.shape, BF16),
            pltpu.VMEM(hops.shape, BF16),
            pltpu.VMEM((chunks, times) + piece, BF16),
            pltpu.VMEM((chunks, times) + piece, F32),
            pltpu.VMEM((exchanges, chunks, times) + piece, BF16),
            pltpu.VMEM((exchanges, chunks, times) + piece, BF16),
            pltpu.VMEM((exchanges, chunks, times) + piece, BF16),
            pltpu.VMEM((exchanges, chunks) + piece, BF16),
            pltpu.VMEM((exchanges, chunks) + piece, BF16),
            dma((chunks, times, sites)),
            dma((times, sites)),
            dma(()),
            dma(()),
            per_piece, per_piece, per_piece, per_piece,
            per_chunk, per_chunk, per_chunk, per_chunk,
        ],
        compiler_params=pltpu.CompilerParams(collective_id=0, has_side_effects=True),
        name="sweeps",
    )(fine, basis, diag, hops, table.T, agg)
    cells = pltpu.with_memory_space_constraint(cells, pltpu.VMEM)
    basis = pltpu.with_memory_space_constraint(basis, pltpu.VMEM)
    return pl.pallas_call(
        prolong_kernel,
        out_shape=jax.ShapeDtypeStruct(fine.shape, BF16),
        in_specs=[smem_spec, vmem_spec, vmem_spec],
        out_specs=any_spec,
        scratch_shapes=[pltpu.VMEM(fine.shape, BF16), dma((times, sites, STORES))],
        name="prolong",
    )(agg, cells, basis)


def solution(mesh):
    return jax.shard_map(
        functools.partial(body, mesh.shape["lat"], mesh.shape["src"]),
        mesh=mesh,
        in_specs=(
            P("lat", "src", None, None),
            P("lat", "src", None, None),
            P("lat", "src", None, None),
            P("lat", "src", None, None, None),
            P(),
            P("lat", "src"),
        ),
        out_specs=P("lat", "src", None, None),
        check_vma=False,
    )
```

profile of v0, /device:TPU:0, one launch (start us, length us, event | category | flops | bytes accessed | tf_op | source)
XLA Modules:
  0.0 29.9 jit_solution(4046740979413470455)
XLA Ops:
  0.0 26.8 %sweeps.1 = (bf16[2,2,256,128]{3,2,1,0:T(8,128)(2,1)S(1)}, bf16[2,2,2048,128]{3,2,1,0:T(8,128)(2,1)S(1)}) custom-call(bf16[2,2,256,2048]{3,2,1,0:T(8,128)(2,1)} %fine.1, bf16[2,2,2048,128]{3,2,1,0:T(8,128)(2,1)} %basis.1, bf16[2,2,128,128]{3,2,1,0:T(8,128)(2,1)} %diag.1, bf16[2,2,8,128,128]{4,3,2,1,0:T(8,128)(2,1)} %hops.1, s32[6,16]{1,0:T(8,128)} %bitcast.1, ...), custom_call_target="tpu_custom_call" | custom-call | tf_op jit(solution)/shard_map/sweeps/pallas_call | solution.py:210
  26.8 3.1 %prolong.1 = bf16[2,2,256,2048]{3,2,1,0:T(8,128)(2,1)} custom-call(s32[2,2]{1,0:T(2,128)} %agg.3, bf16[2,2,256,128]{3,2,1,0:T(8,128)(2,1)S(1)} %get-tuple-element.7.cells, bf16[2,2,2048,128]{3,2,1,0:T(8,128)(2,1)S(1)} %get-tuple-element.8.basis), custom_call_target="tpu_custom_call" | custom-call | tf_op jit(solution)/shard_map/prolong/pallas_call | solution.py:238
where the time goes:
time: 30.1 us; the launch traced here: 29.9 us
  Pallas kernels  29.8 us (99%)
    pallas_call x1, Pallas kernels, body(): pl.pallas_call(functools.partial(sweep_kernel, chunks, lats, srcs), out_s...  26.8 us
    pallas_call x1, Pallas kernels, body(): pl.pallas_call(prolong_kernel, out_shape=jax.ShapeDtypeStruct(fine.shape,...  3.06 us

commit v1 on v0

v1 whole, which is shorter than its diff:
```python
import functools
import math

import jax
import jax.numpy as jnp
from jax import lax
from jax.experimental import pallas as pl
from jax.experimental.pallas import tpu as pltpu
from jax.sharding import PartitionSpec as P

SWEEPS = 3
DAMPING = 0.8
CHUNKS = 4
BLOCKS = (1, 1, 2)
VMEM_BYTES = 67043328
CROSS_BLOCK = 1
HEAD = 2
FORWARD_AT = (0.0, 5.0)
FINISH_AT = (2.4, 7.4)
LOCAL_AT = (-1.0, 2.5)
F32 = jnp.float32
BF16 = jnp.bfloat16


def dot(a, b):
    return jnp.dot(a, b, preferred_element_type=F32)


def timetable(times, sites):
    steps = []
    for c in range(CHUNKS):
        for x in range(SWEEPS - 1):
            steps.append((FORWARD_AT[x] + c, 0, "forward", x, c))
            steps.append((LOCAL_AT[x] + c, 1, "local", x, c))
            steps.append((FINISH_AT[x] + c, 2, "finish", x, c))
    count = times * sites
    for n in range(count):
        steps.append((FINISH_AT[-1] + HEAD - 1 + n * (CHUNKS - HEAD) / count, 3, "prolong", n // sites, n % sites))
    return [step[2:] for step in sorted(steps)]


def sweep_kernel(
    lats, srcs, fine, basis, diag, hops, table_h, agg_h, last, basis_v, out_v,
    table, agg, table_sem, agg_sem, fine_v, diag_v, hops_v, rhs, acc, cells, from_partner, from_far, above, below,
    fine_sem, basis_sem, diag_sem, hops_sem,
    partner_send, partner_recv, far_send, far_recv, above_send, above_recv, below_send, below_recv,
    far_ready, cross_ready,
):
    times, sites, sources, _ = fine.shape
    width = basis.shape[3]
    rows = sources // CHUNKS
    lat, src = lax.axis_index("lat"), lax.axis_index("src")
    later, earlier = lax.rem(lat + 1, lats), lax.rem(lat + lats - 1, lats)
    odd = lax.rem(src, 2)
    partner = src + 1 - 2 * odd
    far_target = lax.rem(src + 2 - 4 * odd + srcs, srcs)
    mate = lat + 1 - 2 * lax.rem(lat, 2)
    cross = lax.rem(lat - 1 + 2 * lax.rem(lat, 2) + lats, lats)
    up, down = lax.rem(src + 2, srcs), lax.rem(src - 2 + srcs, srcs)
    first_of_cross = lat < cross
    barrier = pltpu.get_barrier_semaphore()

    def signal(semaphore, device):
        pl.semaphore_signal(semaphore, inc=1, device_id=device, device_id_type=pl.DeviceIdType.MESH)

    signal(barrier, (lat, down))
    signal(barrier, (lat, partner))
    signal(barrier, (mate, src))

    def meet():
        pl.semaphore_wait(barrier, jnp.where(first_of_cross, 3, 4))

        @pl.when(odd == 1)
        def _():
            signal(far_ready, (lat, up))

        @pl.when(jnp.logical_not(first_of_cross))
        def _():
            signal(cross_ready, (cross, src))

    spans = []
    for b, n in enumerate(BLOCKS):
        spans.append((sum(BLOCKS[:b]), n))

    def load_fine(b, t, s):
        first, n = spans[b]
        span = pl.ds(first * rows, n * rows)
        return pltpu.make_async_copy(fine.at[t, s, span], fine_v.at[t, s, span], fine_sem.at[b, t, s])

    def load_basis(t, s):
        return pltpu.make_async_copy(basis.at[t, s], basis_v.at[t, s], basis_sem.at[t, s])

    load_table = pltpu.make_async_copy(table_h, table, table_sem)
    load_agg = pltpu.make_async_copy(agg_h, agg, agg_sem)
    load_diag = pltpu.make_async_copy(diag, diag_v, diag_sem)
    load_hops = pltpu.make_async_copy(hops, hops_v, hops_sem)

    def start_block(b):
        for t in range(times):
            for s in range(sites):
                if b == 0:
                    load_basis(t, s).start()
                load_fine(b, t, s).start()
            if b == 0 and t == 0:
                load_diag.start()

    start_block(0)
    load_agg.start()
    load_table.start()

    @pl.when(first_of_cross)
    def _():
        signal(barrier, (cross, src))

    for b in range(1, len(BLOCKS)):
        start_block(b)
        if b == 1:
            load_hops.start()

    def remote(source, target, send, recv, device):
        return pltpu.make_async_remote_copy(
            src_ref=source, dst_ref=target, send_sem=send, recv_sem=recv,
            device_id=device, device_id_type=pl.DeviceIdType.MESH)

    def to_partner(x, c):
        return remote(cells.at[x, c], from_partner.at[x, c],
                      partner_send.at[x, c], partner_recv.at[x, c], (lat, partner))

    def to_far(x, c):
        return remote(from_partner.at[x, c], from_far.at[x, c],
                      far_send.at[x, c], far_recv.at[x, c], (lat, far_target))

    def to_later(x, c):
        return remote(cells.at[x, c, times - 1], below.at[x, c],
                      below_send.at[x, c], below_recv.at[x, c], (later, src))

    def to_earlier(x, c):
        return remote(cells.at[x, c, 0], above.at[x, c],
                      above_send.at[x, c], above_recv.at[x, c], (earlier, src))

    def send_time(x, c):
        to_later(x, c).start()
        to_earlier(x, c).start()

    def exchanged(t, values):
        swap = lax.rem(agg[t, 0], sites) == 1
        return [jnp.where(swap, values[1 - s], values[s]) for s in range(sites)]

    def restrict(b):
        first, n = spans[b]
        span = pl.ds(first * rows, n * rows)
        for t in range(times):
            for s in range(sites):
                if b == 0:
                    load_basis(t, s).wait()
                load_fine(b, t, s).wait()
        if b == 0:
            load_diag.wait()
            load_agg.wait()
        coarse = [[dot(fine_v[t, s, span], basis_v[t, s]) for s in range(sites)] for t in range(times)]
        here = [exchanged(t, [value.astype(BF16) for value in coarse[t]]) for t in range(times)]
        applied = [[dot(here[t][s], diag_v[t, s]) for s in range(sites)] for t in range(times)]
        for t in range(times):
            for s in range(sites):
                start = (DAMPING * applied[t][s]).astype(BF16)
                for i in range(n):
                    part = slice(i * rows, (i + 1) * rows)
                    cells[0, first + i, t, s] = start[part]
                    rhs[first + i, t, s] = here[t][s][part]
        if b == 0:
            meet()
        for i in range(n):
            to_partner(0, first + i).start()

    sent = 0
    for b in range(len(BLOCKS)):
        restrict(b)
        if b == CROSS_BLOCK:

            @pl.when(first_of_cross)
            def _():
                pl.semaphore_wait(cross_ready, 1)

        if b >= CROSS_BLOCK:
            for c in range(sent, spans[b][0] + spans[b][1]):
                send_time(0, c)
            sent = spans[b][0] + spans[b][1]
    load_table.wait()
    load_hops.wait()

    partner_first = [table[0, src * sites + s] == partner * sites + s for s in range(sites)]

    def local(x, c):
        for t in range(times):
            for s in range(sites):
                own, other = cells[x, c, t, s], cells[x, c, t, 1 - s]
                total = dot(jnp.concatenate([own, own], axis=1), hops_v[t, s, 2:4].reshape(-1, width))
                total += dot(jnp.concatenate([other, other], axis=1), hops_v[t, s, 4:6].reshape(-1, width))
                if t + 1 < times:
                    total += dot(cells[x, c, t + 1, s], hops_v[t, s, 6])
                if t > 0:
                    total += dot(cells[x, c, t - 1, s], hops_v[t, s, 7])
                acc[c, t, s] = rhs[c, t, s].astype(F32) - total

    def forward(x, c):
        to_partner(x, c).wait_recv()
        if x == 0 and c == 0:

            @pl.when(odd == 1)
            def _():
                pl.semaphore_wait(far_ready, 1)

        to_far(x, c).start()

    def finish(x, c):
        to_earlier(x, c).wait_recv()
        to_later(x, c).wait_recv()
        to_far(x, c).wait_recv()
        blocks = [(t, s) for t in range(times) for s in range(sites)]
        totals = {}
        for t, s in blocks:
            near, far = from_partner[x, c, t, s], from_far[x, c, t, s]
            pair = jnp.concatenate(
                [jnp.where(partner_first[s], near, far), jnp.where(partner_first[s], far, near)], axis=1)
            totals[t, s] = dot(pair, hops_v[t, s, 0:2].reshape(-1, width))
            if t == times - 1:
                totals[t, s] += dot(above[x, c, s], hops_v[t, s, 6])
            if t == 0:
                totals[t, s] += dot(below[x, c, s], hops_v[t, s, 7])
        differences = {(t, s): (acc[c, t, s] - totals[t, s]).astype(BF16) for t, s in blocks}
        applied = {(t, s): dot(differences[t, s], diag_v[t, s]) for t, s in blocks}
        new = {
            (t, s): ((1.0 - DAMPING) * cells[x, c, t, s].astype(F32) + DAMPING * applied[t, s]).astype(BF16)
            for t, s in blocks
        }
        if x + 1 < SWEEPS - 1:
            for t in range(times):
                for s in range(sites):
                    cells[x + 1, c, t, s] = new[t, s]
            to_partner(x + 1, c).start()
            send_time(x + 1, c)
        else:
            for t in range(times):
                gathered = exchanged(t, [new[t, s] for s in range(sites)])
                for s in range(sites):
                    last[t, s, pl.ds(c * rows, rows)] = gathered[s]

    def prolong(t, s):
        span = pl.ds(0, HEAD * rows)
        out_v[t, s, span] = lax.dot_general(
            last[t, s, span], basis_v[t, s], (((1,), (1,)), ((), ())), preferred_element_type=F32).astype(BF16)

    actions = {"forward": forward, "local": local, "finish": finish, "prolong": prolong}
    for name, *at in timetable(times, sites):
        actions[name](*at)

    for c in range(CHUNKS):
        for x in range(SWEEPS - 1):
            to_partner(x, c).wait_send()
            to_far(x, c).wait_send()
            to_later(x, c).wait_send()
            to_earlier(x, c).wait_send()


def prolong_kernel(cells, basis, head_v, out, tail_v, head_sem, tail_sem):
    times, sites, sources, _ = cells.shape
    top = HEAD * (sources // CHUNKS)
    head, tail = pl.ds(0, top), pl.ds(top, sources - top)
    blocks = [(t, s) for t in range(times) for s in range(sites)]

    def store_head(t, s):
        return pltpu.make_async_copy(head_v.at[t, s, head], out.at[t, s, head], head_sem.at[t, s])

    def store_tail(t, s):
        return pltpu.make_async_copy(tail_v.at[t, s], out.at[t, s, tail], tail_sem.at[t, s])

    for t, s in blocks:
        store_head(t, s).start()
    for t, s in blocks:
        tail_v[t, s] = lax.dot_general(
            cells[t, s, tail], basis[t, s], (((1,), (1,)), ((), ())), preferred_element_type=F32).astype(BF16)
        store_tail(t, s).start()
    for t, s in blocks:
        store_head(t, s).wait()
        store_tail(t, s).wait()


def body(lats, srcs, fine, basis, diag, hops, table, agg):
    times, sites, sources, depth = fine.shape
    width = basis.shape[3]
    exchanges = SWEEPS - 1
    rows = sources // CHUNKS
    any_spec = pl.BlockSpec(memory_space=pl.ANY)
    vmem_spec = pl.BlockSpec(memory_space=pltpu.VMEM)
    dma = pltpu.SemaphoreType.DMA
    piece = (times, sites, rows, width)
    per_chunk = dma((exchanges, CHUNKS))
    handed = 2 * (times * sites * sources * width + math.prod(basis.shape) + math.prod(fine.shape))
    grant = VMEM_BYTES - handed - 2**18
    cells, basis, head = pl.pallas_call(
        functools.partial(sweep_kernel, lats, srcs),
        out_shape=[
            pltpu.VMEM((times, sites, sources, width), BF16),
            pltpu.VMEM(basis.shape, BF16),
            pltpu.VMEM(fine.shape, BF16),
        ],
        in_specs=[any_spec] * 6,
        out_specs=[vmem_spec] * 3,
        scratch_shapes=[
            pltpu.SMEM(table.shape[::-1], jnp.int32),
            pltpu.SMEM(agg.shape, jnp.int32),
            dma(()),
            dma(()),
            pltpu.VMEM(fine.shape, BF16),
            pltpu.VMEM(diag.shape, BF16),
            pltpu.VMEM(hops.shape, BF16),
            pltpu.VMEM((CHUNKS,) + piece, BF16),
            pltpu.VMEM((CHUNKS,) + piece, F32),
            pltpu.VMEM((exchanges, CHUNKS) + piece, BF16),
            pltpu.VMEM((exchanges, CHUNKS) + piece, BF16),
            pltpu.VMEM((exchanges, CHUNKS) + piece, BF16),
            pltpu.VMEM((exchanges, CHUNKS) + piece[1:], BF16),
            pltpu.VMEM((exchanges, CHUNKS) + piece[1:], BF16),
            dma((len(BLOCKS), times, sites)),
            dma((times, sites)),
            dma(()),
            dma(()),
            per_chunk, per_chunk, per_chunk, per_chunk,
            per_chunk, per_chunk, per_chunk, per_chunk,
            pltpu.SemaphoreType.REGULAR,
            pltpu.SemaphoreType.REGULAR,
        ],
        compiler_params=pltpu.CompilerParams(collective_id=0, has_side_effects=True, vmem_limit_bytes=grant),
        name="sweeps",
    )(fine, basis, diag, hops, table.T, agg)
    cells = pltpu.with_memory_space_constraint(cells, pltpu.VMEM)
    basis = pltpu.with_memory_space_constraint(basis, pltpu.VMEM)
    head = pltpu.with_memory_space_constraint(head, pltpu.VMEM)
    top = HEAD * rows
    return pl.pallas_call(
        prolong_kernel,
        out_shape=jax.ShapeDtypeStruct(fine.shape, BF16),
        in_specs=[vmem_spec] * 3,
        out_specs=any_spec,
        scratch_shapes=[
            pltpu.VMEM((times, sites, sources - top, depth), BF16),
            dma((times, sites)),
            dma((times, sites)),
        ],
        compiler_params=pltpu.CompilerParams(vmem_limit_bytes=grant),
        name="prolong",
    )(cells, basis, head)


def solution(mesh):
    return jax.shard_map(
        functools.partial(body, mesh.shape["lat"], mesh.shape["src"]),
        mesh=mesh,
        in_specs=(
            P("lat", "src", None, None),
            P("lat", "src", None, None),
            P("lat", "src", None, None),
            P("lat", "src", None, None, None),
            P(),
            P("lat", "src"),
        ),
        out_specs=P("lat", "src", None, None),
        check_vma=False,
    )
```

time: 30.1 us -> 28 us (0.930)
  Pallas kernels: 29.8 us -> 27.8 us
    pallas_call x1, Pallas kernels: 26.8 us -> 25.8 us  [body(): pl.pallas_call(functools.partial(sweep_kernel, lats, srcs), out_shape=[pl...]
    pallas_call x1, Pallas kernels: 3.06 us -> 2.07 us  [body(): pl.pallas_call(prolong_kernel, out_shape=jax.ShapeDtypeStruct(fine.shape,...]
where the time goes in v1:
time: 28 us; the launch traced here: 27.9 us
  Pallas kernels  27.8 us (99%)
    pallas_call x1, Pallas kernels, body(): pl.pallas_call(functools.partial(sweep_kernel, lats, srcs), out_shape=[pl...  25.8 us
    pallas_call x1, Pallas kernels, body(): pl.pallas_call(prolong_kernel, out_shape=jax.ShapeDtypeStruct(fine.shape,...  2.07 us

profile of v1, /device:TPU:0, one launch (start us, length us, event | category | flops | bytes accessed | tf_op | source)
XLA Modules:
  0.0 27.9 jit_solution(4754435641467872592)
XLA Ops:
  0.0 25.8 %sweeps.1 = (bf16[2,2,256,128]{3,2,1,0:T(8,128)(2,1)S(1)}, bf16[2,2,2048,128]{3,2,1,0:T(8,128)(2,1)S(1)}, bf16[2,2,256,2048]{3,2,1,0:T(8,128)(2,1)S(1)}) custom-call(bf16[2,2,256,2048]{3,2,1,0:T(8,128)(2,1)} %fine.1, bf16[2,2,2048,128]{3,2,1,0:T(8,128)(2,1)} %basis.1, bf16[2,2,128,128]{3,2,1,0:T(8,128)(2,1)} %diag.1, bf16[2,2,8,128,128]{4,3,2,1,0:T(8,128)(2,1)} %hops.1, ...), custom_call_target="tpu_custom_call" | custom-call | tf_op jit(solution)/shard_map/sweeps/pallas_call | solution.py:300
  25.8 2.1 %prolong.1 = bf16[2,2,256,2048]{3,2,1,0:T(8,128)(2,1)} custom-call(bf16[2,2,256,128]{3,2,1,0:T(8,128)(2,1)S(1)} %get-tuple-element.8.cells, bf16[2,2,2048,128]{3,2,1,0:T(8,128)(2,1)S(1)} %get-tuple-element.9.basis, bf16[2,2,256,2048]{3,2,1,0:T(8,128)(2,1)S(1)} %get-tuple-element.10.head_v), custom_call_target="tpu_custom_call" | custom-call | tf_op jit(solution)/shard_map/prolong/pallas_call | solution.py:340

commit v2 on v1

--- a/solution.py
+++ b/solution.py
@@ -10,32 +10,46 @@
 
 SWEEPS = 3
 DAMPING = 0.8
-CHUNKS = 4
+SIZES = (2, 2, 2, 2)
+UNITS = sum(SIZES)
+CHUNKS = len(SIZES)
 BLOCKS = (1, 1, 2)
 VMEM_BYTES = 67043328
+DIRECT = 2
 CROSS_BLOCK = 1
 HEAD = 2
-FORWARD_AT = (0.0, 5.0)
-FINISH_AT = (2.4, 7.4)
-LOCAL_AT = (-1.0, 2.5)
+LAG = (3.8, 2.8)
+SHIFT = 10.0
 F32 = jnp.float32
 BF16 = jnp.bfloat16
 
 
 def dot(a, b):
     return jnp.dot(a, b, preferred_element_type=F32)
+
+
+def first_unit(c):
+    return sum(SIZES[:c])
 
 
 def timetable(times, sites):
     steps = []
     for c in range(CHUNKS):
+        end = first_unit(c + 1)
         for x in range(SWEEPS - 1):
-            steps.append((FORWARD_AT[x] + c, 0, "forward", x, c))
-            steps.append((LOCAL_AT[x] + c, 1, "local", x, c))
-            steps.append((FINISH_AT[x] + c, 2, "finish", x, c))
+            forward = end + SHIFT * x
+            finish = forward + SIZES[c] + LAG[x]
+            steps.append((forward, 0, "forward", x, c))
+            steps.append((finish, 2, "finish", x, c))
+            if x == 0:
+                steps.append((end - 4.0, 1, "local", 0, c))
+            if x + 1 < SWEEPS - 1:
+                steps.append((finish + 0.2, 1, "local", x + 1, c))
+            if x == SWEEPS - 2 and c == HEAD - 1:
+                ready = finish
     count = times * sites
     for n in range(count):
-        steps.append((FINISH_AT[-1] + HEAD - 1 + n * (CHUNKS - HEAD) / count, 3, "prolong", n // sites, n % sites))
+        steps.append((ready + n * (UNITS - first_unit(HEAD)) / count, 3, "prolong", n // sites, n % sites))
     return [step[2:] for step in sorted(steps)]
 
 
@@ -44,11 +58,11 @@
     table, agg, table_sem, agg_sem, fine_v, diag_v, hops_v, rhs, acc, cells, from_partner, from_far, above, below,
     fine_sem, basis_sem, diag_sem, hops_sem,
     partner_send, partner_recv, far_send, far_recv, above_send, above_recv, below_send, below_recv,
-    far_ready, cross_ready,
+    direct_send, far_ready, cross_ready,
 ):
     times, sites, sources, _ = fine.shape
     width = basis.shape[3]
-    rows = sources // CHUNKS
+    rows = sources // UNITS
     lat, src = lax.axis_index("lat"), lax.axis_index("src")
     later, earlier = lax.rem(lat + 1, lats), lax.rem(lat + lats - 1, lats)
     odd = lax.rem(src, 2)
@@ -80,11 +94,11 @@
 
     spans = []
     for b, n in enumerate(BLOCKS):
-        spans.append((sum(BLOCKS[:b]), n))
+        start = sum(BLOCKS[:b])
+        spans.append((start, n, pl.ds(first_unit(start) * rows, sum(SIZES[start:start + n]) * rows)))
 
     def load_fine(b, t, s):
-        first, n = spans[b]
-        span = pl.ds(first * rows, n * rows)
+        span = spans[b][2]
         return pltpu.make_async_copy(fine.at[t, s, span], fine_v.at[t, s, span], fine_sem.at[b, t, s])
 
     def load_basis(t, s):
@@ -122,20 +136,33 @@
             src_ref=source, dst_ref=target, send_sem=send, recv_sem=recv,
             device_id=device, device_id_type=pl.DeviceIdType.MESH)
 
+    def units(c):
+        return pl.ds(first_unit(c), SIZES[c])
+
     def to_partner(x, c):
-        return remote(cells.at[x, c], from_partner.at[x, c],
+        return remote(cells.at[x, units(c)], from_partner.at[x, units(c)],
                       partner_send.at[x, c], partner_recv.at[x, c], (lat, partner))
 
     def to_far(x, c):
-        return remote(from_partner.at[x, c], from_far.at[x, c],
+        return remote(from_partner.at[x, units(c)], from_far.at[x, units(c)],
                       far_send.at[x, c], far_recv.at[x, c], (lat, far_target))
 
+    relays = far_target != 0
+    is_last = src == srcs - 1
+
+    def to_first(x, c):
+        return remote(cells.at[x, units(c)], from_far.at[x, units(c)],
+                      direct_send.at[x, c], far_recv.at[x, c], (lat, 0))
+
+    def direct(x, c):
+        return x == SWEEPS - 2 and c >= CHUNKS - DIRECT
+
     def to_later(x, c):
-        return remote(cells.at[x, c, times - 1], below.at[x, c],
+        return remote(cells.at[x, units(c), times - 1], below.at[x, units(c)],
                       below_send.at[x, c], below_recv.at[x, c], (later, src))
 
     def to_earlier(x, c):
-        return remote(cells.at[x, c, 0], above.at[x, c],
+        return remote(cells.at[x, units(c), 0], above.at[x, units(c)],
                       above_send.at[x, c], above_recv.at[x, c], (earlier, src))
 
     def send_time(x, c):
@@ -147,8 +174,7 @@
         return [jnp.where(swap, values[1 - s], values[s]) for s in range(sites)]
 
     def restrict(b):
-        first, n = spans[b]
-        span = pl.ds(first * rows, n * rows)
+        first, n, span = spans[b]
         for t in range(times):
             for s in range(sites):
                 if b == 0:
@@ -163,10 +189,9 @@
         for t in range(times):
             for s in range(sites):
                 start = (DAMPING * applied[t][s]).astype(BF16)
-                for i in range(n):
-                    part = slice(i * rows, (i + 1) * rows)
-                    cells[0, first + i, t, s] = start[part]
-                    rhs[first + i, t, s] = here[t][s][part]
+                at = pl.ds(first_unit(first), sum(SIZES[first:first + n]))
+                cells[0, at, t, s] = start.reshape(-1, rows, width)
+                rhs[at, t, s] = here[t][s].reshape(-1, rows, width)
         if b == 0:
             meet()
         for i in range(n):
@@ -182,25 +207,30 @@
                 pl.semaphore_wait(cross_ready, 1)
 
         if b >= CROSS_BLOCK:
-            for c in range(sent, spans[b][0] + spans[b][1]):
+            done = spans[b][0] + spans[b][1]
+            for c in range(sent, done):
                 send_time(0, c)
-            sent = spans[b][0] + spans[b][1]
+            sent = done
     load_table.wait()
     load_hops.wait()
 
     partner_first = [table[0, src * sites + s] == partner * sites + s for s in range(sites)]
 
+    def flat(value):
+        return value.reshape(-1, width)
+
     def local(x, c):
+        at = units(c)
         for t in range(times):
             for s in range(sites):
-                own, other = cells[x, c, t, s], cells[x, c, t, 1 - s]
+                own, other = flat(cells[x, at, t, s]), flat(cells[x, at, t, 1 - s])
                 total = dot(jnp.concatenate([own, own], axis=1), hops_v[t, s, 2:4].reshape(-1, width))
                 total += dot(jnp.concatenate([other, other], axis=1), hops_v[t, s, 4:6].reshape(-1, width))
                 if t + 1 < times:
-                    total += dot(cells[x, c, t + 1, s], hops_v[t, s, 6])
+                    total += dot(flat(cells[x, at, t + 1, s]), hops_v[t, s, 6])
                 if t > 0:
-                    total += dot(cells[x, c, t - 1, s], hops_v[t, s, 7])
-                acc[c, t, s] = rhs[c, t, s].astype(F32) - total
+                    total += dot(flat(cells[x, at, t - 1, s]), hops_v[t, s, 7])
+                acc[at, t, s] = (flat(rhs[at, t, s]).astype(F32) - total).reshape(-1, rows, width)
 
     def forward(x, c):
         to_partner(x, c).wait_recv()
@@ -210,43 +240,49 @@
             def _():
                 pl.semaphore_wait(far_ready, 1)
 
-        to_far(x, c).start()
+        if direct(x, c):
+            pl.when(relays)(lambda: to_far(x, c).start())
+        else:
+            to_far(x, c).start()
 
     def finish(x, c):
         to_earlier(x, c).wait_recv()
         to_later(x, c).wait_recv()
         to_far(x, c).wait_recv()
+        at = units(c)
         blocks = [(t, s) for t in range(times) for s in range(sites)]
         totals = {}
         for t, s in blocks:
-            near, far = from_partner[x, c, t, s], from_far[x, c, t, s]
+            near, far = flat(from_partner[x, at, t, s]), flat(from_far[x, at, t, s])
             pair = jnp.concatenate(
                 [jnp.where(partner_first[s], near, far), jnp.where(partner_first[s], far, near)], axis=1)
             totals[t, s] = dot(pair, hops_v[t, s, 0:2].reshape(-1, width))
             if t == times - 1:
-                totals[t, s] += dot(above[x, c, s], hops_v[t, s, 6])
+                totals[t, s] += dot(flat(above[x, at, s]), hops_v[t, s, 6])
             if t == 0:
-                totals[t, s] += dot(below[x, c, s], hops_v[t, s, 7])
-        differences = {(t, s): (acc[c, t, s] - totals[t, s]).astype(BF16) for t, s in blocks}
+                totals[t, s] += dot(flat(below[x, at, s]), hops_v[t, s, 7])
+        differences = {(t, s): (flat(acc[at, t, s]) - totals[t, s]).astype(BF16) for t, s in blocks}
         applied = {(t, s): dot(differences[t, s], diag_v[t, s]) for t, s in blocks}
         new = {
-            (t, s): ((1.0 - DAMPING) * cells[x, c, t, s].astype(F32) + DAMPING * applied[t, s]).astype(BF16)
+            (t, s): ((1.0 - DAMPING) * flat(cells[x, at, t, s]).astype(F32) + DAMPING * applied[t, s]).astype(BF16)
             for t, s in blocks
         }
         if x + 1 < SWEEPS - 1:
             for t in range(times):
                 for s in range(sites):
-                    cells[x + 1, c, t, s] = new[t, s]
+                    cells[x + 1, at, t, s] = new[t, s].reshape(-1, rows, width)
+            if direct(x + 1, c):
+                pl.when(is_last)(lambda: to_first(x + 1, c).start())
             to_partner(x + 1, c).start()
             send_time(x + 1, c)
         else:
             for t in range(times):
                 gathered = exchanged(t, [new[t, s] for s in range(sites)])
                 for s in range(sites):
-                    last[t, s, pl.ds(c * rows, rows)] = gathered[s]
+                    last[t, s, pl.ds(first_unit(c) * rows, SIZES[c] * rows)] = gathered[s]
 
     def prolong(t, s):
-        span = pl.ds(0, HEAD * rows)
+        span = pl.ds(0, first_unit(HEAD) * rows)
         out_v[t, s, span] = lax.dot_general(
             last[t, s, span], basis_v[t, s], (((1,), (1,)), ((), ())), preferred_element_type=F32).astype(BF16)
 
@@ -257,14 +293,18 @@
     for c in range(CHUNKS):
         for x in range(SWEEPS - 1):
             to_partner(x, c).wait_send()
-            to_far(x, c).wait_send()
+            if direct(x, c):
+                pl.when(relays)(lambda: to_far(x, c).wait_send())
+                pl.when(is_last)(lambda: to_first(x, c).wait_send())
+            else:
+                to_far(x, c).wait_send()
             to_later(x, c).wait_send()
             to_earlier(x, c).wait_send()
 
 
 def prolong_kernel(cells, basis, head_v, out, tail_v, head_sem, tail_sem):
     times, sites, sources, _ = cells.shape
-    top = HEAD * (sources // CHUNKS)
+    top = first_unit(HEAD) * (sources // UNITS)
     head, tail = pl.ds(0, top), pl.ds(top, sources - top)
     blocks = [(t, s) for t in range(times) for s in range(sites)]
 
@@ -289,7 +329,7 @@
     times, sites, sources, depth = fine.shape
     width = basis.shape[3]
     exchanges = SWEEPS - 1
-    rows = sources // CHUNKS
+    rows = sources // UNITS
     any_spec = pl.BlockSpec(memory_space=pl.ANY)
     vmem_spec = pl.BlockSpec(memory_space=pltpu.VMEM)
     dma = pltpu.SemaphoreType.DMA
@@ -314,19 +354,20 @@
             pltpu.VMEM(fine.shape, BF16),
             pltpu.VMEM(diag.shape, BF16),
             pltpu.VMEM(hops.shape, BF16),
-            pltpu.VMEM((CHUNKS,) + piece, BF16),
-            pltpu.VMEM((CHUNKS,) + piece, F32),
-            pltpu.VMEM((exchanges, CHUNKS) + piece, BF16),
-            pltpu.VMEM((exchanges, CHUNKS) + piece, BF16),
-            pltpu.VMEM((exchanges, CHUNKS) + piece, BF16),
-            pltpu.VMEM((exchanges, CHUNKS) + piece[1:], BF16),
-            pltpu.VMEM((exchanges, CHUNKS) + piece[1:], BF16),
+            pltpu.VMEM((UNITS,) + piece, BF16),
+            pltpu.VMEM((UNITS,) + piece, F32),
+            pltpu.VMEM((exchanges, UNITS) + piece, BF16),
+            pltpu.VMEM((exchanges, UNITS) + piece, BF16),
+            pltpu.VMEM((exchanges, UNITS) + piece, BF16),
+            pltpu.VMEM((exchanges, UNITS) + piece[1:], BF16),
+            pltpu.VMEM((exchanges, UNITS) + piece[1:], BF16),
             dma((len(BLOCKS), times, sites)),
             dma((times, sites)),
             dma(()),
             dma(()),
             per_chunk, per_chunk, per_chunk, per_chunk,
             per_chunk, per_chunk, per_chunk, per_chunk,
+            dma((exchanges, CHUNKS)),
             pltpu.SemaphoreType.REGULAR,
             pltpu.SemaphoreType.REGULAR,
         ],
@@ -336,7 +377,7 @@
     cells = pltpu.with_memory_space_constraint(cells, pltpu.VMEM)
     basis = pltpu.with_memory_space_constraint(basis, pltpu.VMEM)
     head = pltpu.with_memory_space_constraint(head, pltpu.VMEM)
-    top = HEAD * rows
+    top = first_unit(HEAD) * rows
     return pl.pallas_call(
         prolong_kernel,
         out_shape=jax.ShapeDtypeStruct(fine.shape, BF16),

time: 28 us -> 27.1 us (0.968)
  Pallas kernels: 27.8 us -> 26.9 us
    pallas_call x1, Pallas kernels: 25.8 us -> 24.9 us  [body(): pl.pallas_call(functools.partial(sweep_kernel, lats, srcs), out_shape=[pl...]
where the time goes in v2:
time: 27.1 us; the launch traced here: 26.9 us
  Pallas kernels  26.9 us (99%)
    pallas_call x1, Pallas kernels, body(): pl.pallas_call(functools.partial(sweep_kernel, lats, srcs), out_shape=[pl...  24.9 us
    pallas_call x1, Pallas kernels, body(): pl.pallas_call(prolong_kernel, out_shape=jax.ShapeDtypeStruct(fine.shape,...  2.07 us

profile of v2, /device:TPU:0, one launch (start us, length us, event | category | flops | bytes accessed | tf_op | source)
XLA Modules:
  0.0 26.9 jit_solution(8677359411932346225)
XLA Ops:
  0.0 24.9 %sweeps.1 = (bf16[2,2,256,128]{3,2,1,0:T(8,128)(2,1)S(1)}, bf16[2,2,2048,128]{3,2,1,0:T(8,128)(2,1)S(1)}, bf16[2,2,256,2048]{3,2,1,0:T(8,128)(2,1)S(1)}) custom-call(bf16[2,2,256,2048]{3,2,1,0:T(8,128)(2,1)} %fine.1, bf16[2,2,2048,128]{3,2,1,0:T(8,128)(2,1)} %basis.1, bf16[2,2,128,128]{3,2,1,0:T(8,128)(2,1)} %diag.1, bf16[2,2,8,128,128]{4,3,2,1,0:T(8,128)(2,1)} %hops.1, ...), custom_call_target="tpu_custom_call" | custom-call | tf_op jit(solution)/shard_map/sweeps/pallas_call | solution.py:340
  24.9 2.1 %prolong.1 = bf16[2,2,256,2048]{3,2,1,0:T(8,128)(2,1)} custom-call(bf16[2,2,256,128]{3,2,1,0:T(8,128)(2,1)S(1)} %get-tuple-element.8.cells, bf16[2,2,2048,128]{3,2,1,0:T(8,128)(2,1)S(1)} %get-tuple-element.9.basis, bf16[2,2,256,2048]{3,2,1,0:T(8,128)(2,1)S(1)} %get-tuple-element.10.head_v), custom_call_target="tpu_custom_call" | custom-call | tf_op jit(solution)/shard_map/prolong/pallas_call | solution.py:381

commit v3 on v2

--- a/solution.py
+++ b/solution.py
@@ -18,7 +18,7 @@
 DIRECT = 2
 CROSS_BLOCK = 1
 HEAD = 2
-LAG = (3.8, 2.8)
+LAG = (2.8, 2.8)
 SHIFT = 10.0
 F32 = jnp.float32
 BF16 = jnp.bfloat16
@@ -55,7 +55,7 @@
 
 def sweep_kernel(
     lats, srcs, fine, basis, diag, hops, table_h, agg_h, last, basis_v, out_v,
-    table, agg, table_sem, agg_sem, fine_v, diag_v, hops_v, rhs, acc, cells, from_partner, from_far, above, below,
+    table, agg, table_sem, agg_sem, fine_v, diag_v, hops_v, rhs, acc, remote_v, cells, from_partner, from_far, above, below,
     fine_sem, basis_sem, diag_sem, hops_sem,
     partner_send, partner_recv, far_send, far_recv, above_send, above_recv, below_send, below_recv,
     direct_send, far_ready, cross_ready,
@@ -216,11 +216,21 @@
 
     partner_first = [table[0, src * sites + s] == partner * sites + s for s in range(sites)]
 
+    def prepare():
+        for t in range(times):
+            for s in range(sites):
+                own = diag_v[t, s]
+                columns = [0, 1] + ([6] if t == times - 1 else []) + ([7] if t == 0 else [])
+                for i, k in enumerate(columns):
+                    remote_v[t, s, i] = (DAMPING * dot(hops_v[t, s, k], own)).astype(BF16)
+
     def flat(value):
         return value.reshape(-1, width)
 
     def local(x, c):
         at = units(c)
+        blocks = [(t, s) for t in range(times) for s in range(sites)]
+        totals = {}
         for t in range(times):
             for s in range(sites):
                 own, other = flat(cells[x, at, t, s]), flat(cells[x, at, t, 1 - s])
@@ -230,7 +240,11 @@
                     total += dot(flat(cells[x, at, t + 1, s]), hops_v[t, s, 6])
                 if t > 0:
                     total += dot(flat(cells[x, at, t - 1, s]), hops_v[t, s, 7])
-                acc[at, t, s] = (flat(rhs[at, t, s]).astype(F32) - total).reshape(-1, rows, width)
+                totals[t, s] = (flat(rhs[at, t, s]).astype(F32) - total).astype(BF16)
+        for t, s in blocks:
+            applied = dot(totals[t, s], diag_v[t, s])
+            kept = (1.0 - DAMPING) * flat(cells[x, at, t, s]).astype(F32) + DAMPING * applied
+            acc[at, t, s] = kept.reshape(-1, rows, width)
 
     def forward(x, c):
         to_partner(x, c).wait_recv()
@@ -251,22 +265,19 @@
         to_far(x, c).wait_recv()
         at = units(c)
         blocks = [(t, s) for t in range(times) for s in range(sites)]
-        totals = {}
+        new = {}
         for t, s in blocks:
             near, far = flat(from_partner[x, at, t, s]), flat(from_far[x, at, t, s])
             pair = jnp.concatenate(
                 [jnp.where(partner_first[s], near, far), jnp.where(partner_first[s], far, near)], axis=1)
-            totals[t, s] = dot(pair, hops_v[t, s, 0:2].reshape(-1, width))
+            total = dot(pair, remote_v[t, s, 0:2].reshape(-1, width))
+            i = 2
             if t == times - 1:
-                totals[t, s] += dot(flat(above[x, at, s]), hops_v[t, s, 6])
+                total += dot(flat(above[x, at, s]), remote_v[t, s, i])
+                i += 1
             if t == 0:
-                totals[t, s] += dot(flat(below[x, at, s]), hops_v[t, s, 7])
-        differences = {(t, s): (flat(acc[at, t, s]) - totals[t, s]).astype(BF16) for t, s in blocks}
-        applied = {(t, s): dot(differences[t, s], diag_v[t, s]) for t, s in blocks}
-        new = {
-            (t, s): ((1.0 - DAMPING) * flat(cells[x, at, t, s]).astype(F32) + DAMPING * applied[t, s]).astype(BF16)
-            for t, s in blocks
-        }
+                total += dot(flat(below[x, at, s]), remote_v[t, s, i])
+            new[t, s] = (flat(acc[at, t, s]) - total).astype(BF16)
         if x + 1 < SWEEPS - 1:
             for t in range(times):
                 for s in range(sites):
@@ -287,6 +298,7 @@
             last[t, s, span], basis_v[t, s], (((1,), (1,)), ((), ())), preferred_element_type=F32).astype(BF16)
 
     actions = {"forward": forward, "local": local, "finish": finish, "prolong": prolong}
+    prepare()
     for name, *at in timetable(times, sites):
         actions[name](*at)
 
@@ -356,6 +368,7 @@
             pltpu.VMEM(hops.shape, BF16),
             pltpu.VMEM((UNITS,) + piece, BF16),
             pltpu.VMEM((UNITS,) + piece, F32),
+            pltpu.VMEM(hops.shape[:2] + (4,) + hops.shape[3:], BF16),
             pltpu.VMEM((exchanges, UNITS) + piece, BF16),
             pltpu.VMEM((exchanges, UNITS) + piece, BF16),
             pltpu.VMEM((exchanges, UNITS) + piece, BF16),

time: 27.1 us -> 26.8 us (0.989)
  Pallas kernels: 26.9 us -> 26.6 us
    pallas_call x1, Pallas kernels: 24.9 us -> 24.6 us  [body(): pl.pallas_call(functools.partial(sweep_kernel, lats, srcs), out_shape=[pl...]
where the time goes in v3:
time: 26.8 us; the launch traced here: 26.7 us
  Pallas kernels  26.6 us (99%)
    pallas_call x1, Pallas kernels, body(): pl.pallas_call(functools.partial(sweep_kernel, lats, srcs), out_shape=[pl...  24.6 us
    pallas_call x1, Pallas kernels, body(): pl.pallas_call(prolong_kernel, out_shape=jax.ShapeDtypeStruct(fine.shape,...  2.07 us

profile of v3, /device:TPU:0, one launch (start us, length us, event | category | flops | bytes accessed | tf_op | source)
XLA Modules:
  0.0 26.7 jit_solution(9149731334651710914)
XLA Ops:
  0.0 24.6 %sweeps.1 = (bf16[2,2,256,128]{3,2,1,0:T(8,128)(2,1)S(1)}, bf16[2,2,2048,128]{3,2,1,0:T(8,128)(2,1)S(1)}, bf16[2,2,256,2048]{3,2,1,0:T(8,128)(2,1)S(1)}) custom-call(bf16[2,2,256,2048]{3,2,1,0:T(8,128)(2,1)} %fine.1, bf16[2,2,2048,128]{3,2,1,0:T(8,128)(2,1)} %basis.1, bf16[2,2,128,128]{3,2,1,0:T(8,128)(2,1)} %diag.1, bf16[2,2,8,128,128]{4,3,2,1,0:T(8,128)(2,1)} %hops.1, ...), custom_call_target="tpu_custom_call" | custom-call | tf_op jit(solution)/shard_map/sweeps/pallas_call | solution.py:352
  24.6 2.1 %prolong.1 = bf16[2,2,256,2048]{3,2,1,0:T(8,128)(2,1)} custom-call(bf16[2,2,256,128]{3,2,1,0:T(8,128)(2,1)S(1)} %get-tuple-element.8.cells, bf16[2,2,2048,128]{3,2,1,0:T(8,128)(2,1)S(1)} %get-tuple-element.9.basis, bf16[2,2,256,2048]{3,2,1,0:T(8,128)(2,1)S(1)} %get-tuple-element.10.head_v), custom_call_target="tpu_custom_call" | custom-call | tf_op jit(solution)/shard_map/prolong/pallas_call | solution.py:394

commit v4 on v3

--- a/solution.py
+++ b/solution.py
@@ -19,7 +19,7 @@
 CROSS_BLOCK = 1
 HEAD = 2
 LAG = (2.8, 2.8)
-SHIFT = 10.0
+SHIFT = 9.0
 F32 = jnp.float32
 BF16 = jnp.bfloat16
 

time: 26.8 us -> 26.8 us (level)
  no operation moved by 1% of the time
where the time goes in v4:
time: 26.8 us; the launch traced here: 26.7 us
  Pallas kernels  26.6 us (99%)
    pallas_call x1, Pallas kernels, body(): pl.pallas_call(functools.partial(sweep_kernel, lats, srcs), out_shape=[pl...  24.6 us
    pallas_call x1, Pallas kernels, body(): pl.pallas_call(prolong_kernel, out_shape=jax.ShapeDtypeStruct(fine.shape,...  2.07 us

profile of v4, /device:TPU:0, one launch (start us, length us, event | category | flops | bytes accessed | tf_op | source)
XLA Modules:
  0.0 26.7 jit_solution(14158650207649713999)
XLA Ops:
  0.0 24.6 %sweeps.1 = (bf16[2,2,256,128]{3,2,1,0:T(8,128)(2,1)S(1)}, bf16[2,2,2048,128]{3,2,1,0:T(8,128)(2,1)S(1)}, bf16[2,2,256,2048]{3,2,1,0:T(8,128)(2,1)S(1)}) custom-call(bf16[2,2,256,2048]{3,2,1,0:T(8,128)(2,1)} %fine.1, bf16[2,2,2048,128]{3,2,1,0:T(8,128)(2,1)} %basis.1, bf16[2,2,128,128]{3,2,1,0:T(8,128)(2,1)} %diag.1, bf16[2,2,8,128,128]{4,3,2,1,0:T(8,128)(2,1)} %hops.1, ...), custom_call_target="tpu_custom_call" | custom-call | tf_op jit(solution)/shard_map/sweeps/pallas_call | solution.py:352
  24.6 2.1 %prolong.1 = bf16[2,2,256,2048]{3,2,1,0:T(8,128)(2,1)} custom-call(bf16[2,2,256,128]{3,2,1,0:T(8,128)(2,1)S(1)} %get-tuple-element.8.cells, bf16[2,2,2048,128]{3,2,1,0:T(8,128)(2,1)S(1)} %get-tuple-element.9.basis, bf16[2,2,256,2048]{3,2,1,0:T(8,128)(2,1)S(1)} %get-tuple-element.10.head_v), custom_call_target="tpu_custom_call" | custom-call | tf_op jit(solution)/shard_map/prolong/pallas_call | solution.py:394
